TPU v7x, 512 devices: a whole 4x8x8 slice. The times are simulated.
512 devices in a mesh: vocab: 64 (over y, x, core), width: 8 (over z).
Axes of the slice: x: 4, y: 8, z: 8, core: 2. Of those that a mesh axis runs over, the one named last changes fastest.
Arguments:
- hidden: bfloat16 [8192, 2048], P('vocab', 'width'), may hold values from -400 to 400
- norm_gain: bfloat16 [2048], P('width'), may hold values from 0.5 to 1.5
- head_weight: bfloat16 [102400, 2048], P('vocab', 'width'), may hold values from -1 to 1
- targets: int32 [8192], P(('vocab', 'width')), may hold values from 0 to 102399
- pad_mask: int32 [8192], P(('vocab', 'width')), may hold values 0 or 1
- lengths: int32 [64], replicated, may hold values from 1 to 2048, 8192 in all
Outputs:
- entropy: float32 [8192], P(('vocab', 'width'))
- token_logprob: float32 [8192], P(('vocab', 'width'))
- seq_score: float32 [64], replicated
Inputs may be any that keep to these rules, and one draw needn't show every extreme that they name: The lengths sum to 8192.
All inputs are finite; a program needn't handle non-finite values. No bound on the sum of `pad_mask` on one device may be relied on, other than what follows from the above.
Results may differ from a plain program's by a relative error of at most 0.0031.
Values may be sent and summed in bfloat16 or wider, within the bound.
A program may use at most 64 MiB of HBM per device.

v0:
```python
import math
import jax
import jax.numpy as jnp
from jax import lax
from jax.sharding import PartitionSpec as P

epsilon = 1e-06


def merged_2(value, axis, join):
    pieces = jax.tree.map(lambda part: lax.all_gather(part, axis), value)
    head = jax.tree.map(lambda part: part[0], pieces)
    tail = jax.tree.map(lambda part: part[1:], pieces)
    total, _ = lax.scan(lambda total, piece: (join(total, piece), None), head, tail)
    return total


def summarize(logits, block_ids, first_col):
    peak = jnp.max(logits, axis=1)
    shifted = logits - peak[:, None]
    weights = jnp.exp(shifted)
    exp_total = jnp.sum(weights, axis=1)
    spread = jnp.sum(weights * shifted, axis=1)
    columns = first_col + lax.iota(jnp.int32, logits.shape[1])
    target_logit = jnp.sum(jnp.where(columns[None, :] == block_ids[:, None], logits, 0.0), axis=1)
    return (peak, exp_total, spread, target_logit)


def combine(earlier, later):
    peak = jnp.maximum(earlier[0], later[0])
    left_lift = jnp.exp(earlier[0] - peak)
    right_lift = jnp.exp(later[0] - peak)
    exp_total = earlier[1] * left_lift + later[1] * right_lift
    spread = left_lift * (earlier[2] + (earlier[0] - peak) * earlier[1]) + right_lift * (
        later[2] + (later[0] - peak) * later[1]
    )
    return (peak, exp_total, spread, earlier[3] + later[3])


def per_device(hidden, norm_gain, head_weight, targets, pad_mask, lengths):
    width_count = lax.axis_size("width")
    own_count = targets.shape[0]
    values = hidden.astype(jnp.float32)
    energy = lax.psum(jnp.sum(values * values, axis=1), "width")
    inv_rms = lax.rsqrt(energy / (hidden.shape[1] * width_count) + epsilon)
    normed = (values * inv_rms[:, None] * norm_gain.astype(jnp.float32)[None, :]).astype(
        jnp.bfloat16
    )
    full_rows = lax.all_to_all(normed, "width", split_axis=0, concat_axis=1, tiled=True)
    gathered, gathered_ids = (
        lax.all_gather(full_rows, "vocab", axis=0, tiled=True),
        lax.all_gather(targets, "vocab", axis=0, tiled=True),
    )
    col_count = head_weight.shape[0]
    first_col = lax.axis_index("vocab") * col_count
    total_rows = gathered.shape[0]
    block_rows = math.gcd(total_rows, 512)
    contract = (((1,), (1,)), ((), ()))
    head_full = lax.all_gather(head_weight, "width", axis=1, tiled=True)

    def per_block(inputs):
        logits = lax.dot_general(inputs[0], head_full, contract, preferred_element_type=jnp.float32)
        return summarize(logits, inputs[1], first_col)

    blocked = lax.map(
        per_block,
        (gathered.reshape(-1, block_rows, gathered.shape[1]), gathered_ids.reshape(-1, block_rows)),
    )
    statistics = (
        blocked[0].reshape(-1),
        blocked[1].reshape(-1),
        blocked[2].reshape(-1),
        blocked[3].reshape(-1),
    )
    merged = merged_2(statistics, "vocab", combine)
    own_start = lax.axis_index("vocab") * own_count
    peak = lax.dynamic_slice_in_dim(merged[0], own_start, own_count, 0)
    exp_total = lax.dynamic_slice_in_dim(merged[1], own_start, own_count, 0)
    spread = lax.dynamic_slice_in_dim(merged[2], own_start, own_count, 0)
    target_logit = lax.dynamic_slice_in_dim(merged[3], own_start, own_count, 0)
    kept_mask = pad_mask.astype(jnp.float32)
    log_total = jnp.log(exp_total)
    entropy = kept_mask * (log_total - spread / exp_total)
    token_logprob = kept_mask * (target_logit - peak - log_total)
    device_index = lax.axis_index("vocab") * width_count + lax.axis_index("width")
    token_index = device_index * own_count + lax.iota(jnp.int32, own_count)
    seq_ends = jnp.cumsum(lengths)
    seq_starts = seq_ends - lengths
    member = (
        (token_index[:, None] >= seq_starts[None, :]) & (token_index[:, None] < seq_ends[None, :])
    ).astype(jnp.float32)
    partial_value = jnp.sum(member * token_logprob[:, None], axis=0)
    seq_score = lax.psum(partial_value, ("vocab", "width")) / lengths.astype(jnp.float32)
    return (entropy, token_logprob, seq_score)


def solution(mesh):
    placed = (
        P("vocab", "width"),
        P("width"),
        P("vocab", "width"),
        P(("vocab", "width")),
        P(("vocab", "width")),
        P(),
    )
    return jax.shard_map(
        per_device,
        mesh=mesh,
        in_specs=placed,
        out_specs=(P(("vocab", "width")), P(("vocab", "width")), P()),
        check_vma=False,
    )
```

profile of v0, /device:TPU:1, one launch (start us, length us, event | category | flops | bytes accessed | tf_op | source)
XLA Modules:
  0.0 491.1 jit_solution(4575408305845917003)
XLA Ops:
  7.2 0.0 all-gather.7.cloned.1.call-start
  7.2 0.9 fusion.5
  8.2 20.3 %psum.14 = f32[128]{0:T(128)S(1)} all-reduce(f32[128]{0:T(128)S(1)} %fusion.5), channel_id=1, replica_groups=mesh['vocab'=64,'width'=8] {'width'}, use_global_device_ids=true, to_apply=%region_1.0 | all-reduce | flops 128 | bytes 1024 | tf_op jit(solution)/shard_map/psum | solution.py:44
  28.4 0.7 convert_element_type.18
  29.1 0.9 fusion.7
  30.0 9.6 %all_to_all.19 = bf16[8,16,256]{2,1,0:T(8,128)(2,1)S(1)} all-to-all(bf16[8,16,256]{2,1,0:T(8,128)(2,1)S(1)} %bitcast.73), channel_id=1, replica_groups=mesh['vocab'=64,'width'=8] {'width'}, dimensions={0} | all-to-all | bytes 131072 | tf_op jit(solution)/shard_map/all_to_all | solution.py:49
  39.6 0.6 copy.21
  40.3 0.0 all-gather.9.cloned.1.call-start
  40.3 0.7 all-gather.9.cloned.1.call-update
  41.1 1.3 dynamic-slice
  43.0 0.9 dynamic-update-slice
  43.9 22.5 %all-reduce = s32[1024]{0:T(1024)S(1)} all-reduce(s32[1024]{0:T(1024)S(1)} %dynamic-update-slice), channel_id=1, replica_groups=mesh['vocab'=64,'width'=8] {'vocab'}, use_global_device_ids=true, to_apply=%add | all-reduce | flops 1024 | bytes 8192
  66.4 0.7 copy.16
  67.2 0.1 reduce-window.8
  67.3 0.1 reduce
  67.4 0.7 sub.31
  68.0 58.4 %all-gather.7.cloned.1.call-done = bf16[1024,2048]{1,0:T(8,128)(2,1)} async-done(((bf16[16,2048]{1,0:T(8,128)(2,1)}), bf16[1024,2048]{1,0:T(8,128)(2,1)}) %all-gather.7.cloned.1.call-update) | async-done | bytes 4194320 | tf_op jit(solution)/shard_map/all_gather | solution.py:51
  126.4 83.2 %all-gather.9.cloned.1.call-done = bf16[1600,2048]{1,0:T(8,128)(2,1)} async-done(((bf16[1600,256]{1,0:T(8,128)(2,1)}), bf16[1600,2048]{1,0:T(8,128)(2,1)}) %all-gather.9.cloned.1.call-update) | async-done | bytes 6553616 | tf_op jit(solution)/shard_map/all_gather | solution.py:59
  209.6 16.2 %while.32 = (s32[]{:T(128)}, f32[2,512]{1,0:T(2,128)S(1)}, f32[2,512]{1,0:T(2,128)S(1)}, f32[2,512]{1,0:T(2,128)S(1)}, f32[2,512]{1,0:T(2,128)S(1)}, /*index=5*/...) while((s32[]{:T(128)}, f32[2,512]{1,0:T(2,128)S(1)}, ...), condition=%wide.region_7.8_spmd, body=%wide.region_2.7_spmd.sunk | while | flops 3361996288 | bytes 15250565 | solution.py:65
  209.6 6.4 %fusion.14 = (f32[512]{0:T(512)S(1)}, f32[512,1600]{0,1:T(8,128)S(1)}) fusion(bf16[1600,2048]{1,0:T(8,128)(2,1)} %get-tuple-element.320, bf16[2,512,2048]{2,1,0:T(8,128)(2,1)} %get-tuple-element.319, s32[]{:T(128)} %get-tuple-element.303), kind=kOutput, calls=%fused_computation.31.clone.1 | convolution fusion | flops 3356261888 | bytes 11930112 | tf_op jit(solution)/shard_map/while/body/eval_jaxpr/dot_general | solution.py:62
  216.1 1.4 fusion.15
  217.7 6.4 %fusion.14 = (f32[512]{0:T(512)S(1)}, f32[512,1600]{0,1:T(8,128)S(1)}) fusion(bf16[1600,2048]{1,0:T(8,128)(2,1)} %get-tuple-element.320, bf16[2,512,2048]{2,1,0:T(8,128)(2,1)} %get-tuple-element.319, s32[]{:T(128)} %get-tuple-element.303), kind=kOutput, calls=%fused_computation.31.clone.1 | convolution fusion | flops 3356261888 | bytes 11930112 | tf_op jit(solution)/shard_map/while/body/eval_jaxpr/dot_general | solution.py:62
  224.2 1.4 fusion.15
  225.8 42.7 %all-gather = f32[64,1,1024]{2,1,0:T(1,128)S(1)} all-gather(f32[1,1,1024]{2,1,0:T(1,128)S(1)} %reshape.60), channel_id=1, replica_groups=mesh['vocab'=64,'width'=8] {'vocab'}, dimensions={0}, use_global_device_ids=true | all-gather | bytes 266240 | tf_op jit(solution)/shard_map/all_gather | solution.py:11
  268.6 37.2 %all-gather.1 = f32[64,1,1024]{2,1,0:T(1,128)S(1)} all-gather(f32[1,1,1024]{2,1,0:T(1,128)S(1)} %reshape.62), channel_id=1, replica_groups=mesh['vocab'=64,'width'=8] {'vocab'}, dimensions={0}, use_global_device_ids=true | all-gather | bytes 266240 | tf_op jit(solution)/shard_map/all_gather | solution.py:11
  305.8 36.9 %all-gather.2 = f32[64,1,1024]{2,1,0:T(1,128)S(1)} all-gather(f32[1,1,1024]{2,1,0:T(1,128)S(1)} %reshape.64), channel_id=1, replica_groups=mesh['vocab'=64,'width'=8] {'vocab'}, dimensions={0}, use_global_device_ids=true | all-gather | bytes 266240 | tf_op jit(solution)/shard_map/all_gather | solution.py:11
  342.7 37.1 %all-gather.3 = f32[64,1,1024]{2,1,0:T(1,128)S(1)} all-gather(f32[1,1,1024]{2,1,0:T(1,128)S(1)} %reshape.66), channel_id=1, replica_groups=mesh['vocab'=64,'width'=8] {'vocab'}, dimensions={0}, use_global_device_ids=true | all-gather | bytes 266240 | tf_op jit(solution)/shard_map/all_gather | solution.py:11
  380.2 7.6 %while.33 = (s32[]{:T(128)}, f32[1024]{0:T(1024)S(1)}, f32[1024]{0:T(1024)S(1)}, f32[1024]{0:T(1024)S(1)}, f32[1024]{0:T(1024)S(1)}, /*index=5*/f32[63,1024]{1,0...) while((s32[]{:T(128)}, f32[1024]{0:T(1024)S(1)}, ...), condition=%wide.region_9.10_spmd, body=%wide.region_8.9_spmd.sunk | while | flops 16386 | bytes 110701 | solution.py:14
  387.7 0.6 subtract_multiply_fusion
  388.3 0.1 select_reduce_fusion.1
  388.4 95.3 %psum.15 = f32[64]{0:T(128)S(1)} all-reduce(f32[64]{0:T(128)S(1)} %select_reduce_fusion.1), channel_id=1, replica_groups=mesh['vocab'=64,'width'=8] {'vocab','width'}, use_global_device_ids=true, to_apply=%region_12.13 | all-reduce | flops 64 | bytes 512 | tf_op jit(solution)/shard_map/psum | solution.py:93
  483.7 0.5 convert_divide_fusion
  (421 shorter events, 4.6 us)
Async XLA Ops:
  7.2 119.3 %all-gather.7.cloned.1.call-start = ((), (), s32[]{:S(2)}) async-start(), calls=%async_computation.1 | async-start | bytes 4259840 | tf_op jit(solution)/shard_map/all_gather | solution.py:51
  40.3 169.3 %all-gather.9.cloned.1.call-start = ((), (), s32[]{:S(2)}) async-start(), calls=%async_computation.2 | async-start | bytes 7372800 | tf_op jit(solution)/shard_map/all_gather | solution.py:59
  225.8 162.0 %copy-start.2 = (s32[16]{0:T(128)S(1)}, s32[16]{0:T(128)}, u32[]{:S(2)}) copy-start(s32[16]{0:T(128)} %param.14) | copy-start | bytes 196
  225.8 257.9 %copy-start.1 = (s32[64]{0:T(128)S(1)}, s32[64]{0:T(128)}, u32[]{:S(2)}) copy-start(s32[64]{0:T(128)} %param.15) | copy-start | bytes 772
  388.3 95.9 %copy-start = (f32[16]{0:T(128)}, f32[16]{0:T(128)S(1)}, u32[]{:S(2)}) copy-start(f32[16]{0:T(128)S(1)} %get-tuple-element.158) | copy-start | bytes 196
Sparse Core Ops, SparseCore 0:
  40.4 85.9 all-gather.6
  128.4 81.1 all-gather.8
where the time goes:
time: 491 us
  blocking collectives  302 us (62%)
  waiting for transfers between devices  142 us (29%)
  between operations  14.9 us (3%)
  matrix products  12.9 us (3%)
  other arithmetic  9.19 us (2%)
  local copies, waits for them, and re-layouts  6.36 us (1%)
    all_gather x4, blocking collectives, merged_2(): pieces = jax.tree.map(lambda part: lax.all_gather(part, axis), value)  154 us
    psum x1, blocking collectives, per_device(): lax.psum(partial_value, ('vocab', 'width')) / lengths.astype(jnp.float32)  95.3 us
    all_gather x1, waiting for transfers between devices, per_device(): head_full = lax.all_gather(head_weight, 'width', axis=1, tiled=True)  83.2 us
    all_gather x1, waiting for transfers between devices, per_device(): lax.all_gather(full_rows, 'vocab', axis=0, tiled=True)  58.4 us
    unnamed x1, blocking collectives  22.5 us
    psum x1, blocking collectives, per_device(): energy = lax.psum(jnp.sum(values * values, axis=1), 'width')  20.3 us
    dot_general x2, matrix products, per_block(): lax.dot_general(inputs[0], head_full, contract, preferred_element_type=jn...  12.9 us
  transfers between devices with their start and end apart: 2, of which 2 were waited for; matrix products, arithmetic and copies ran while one was open for 1% of the time, Pallas kernels for 0%

commit v1 on v0

--- a/solution.py
+++ b/solution.py
@@ -5,6 +5,16 @@
 from jax.sharding import PartitionSpec as P
 
 epsilon = 1e-06
+
+
+def gather_by_hops(x, mesh_axis, along):
+    size = lax.axis_size(mesh_axis)
+    moving, blocks = (x, [x])
+    for _ in range(size - 1):
+        moving = lax.ppermute(moving, mesh_axis, [(i, (i + 1) % size) for i in range(size)])
+        blocks.insert(0, moving)
+    line = jnp.concatenate(blocks, axis=along)
+    return jnp.roll(line, (lax.axis_index(mesh_axis) + 1) * x.shape[along], axis=along)
 
 
 def merged_2(value, axis, join):
@@ -56,7 +66,7 @@
     total_rows = gathered.shape[0]
     block_rows = math.gcd(total_rows, 512)
     contract = (((1,), (1,)), ((), ()))
-    head_full = lax.all_gather(head_weight, "width", axis=1, tiled=True)
+    head_full = gather_by_hops(head_weight, "width", 1)
 
     def per_block(inputs):
         logits = lax.dot_general(inputs[0], head_full, contract, preferred_element_type=jnp.float32)

time: 491 us -> 465 us (0.947)
  waiting for transfers between devices: 142 us -> 65.6 us
  starting transfers between devices: 0.08 us -> 19.6 us
  local copies, waits for them, and re-layouts: 6.36 us -> 21.4 us
  blocking collectives: 302 us -> 317 us
    all_gather x1 -> x0, waiting for transfers between devices: 83.2 us -> none  [per_device(): head_full = lax.all_gather(head_weight, 'width', axis=1, tiled=True)]
    ppermute x0 -> x7, waiting for transfers between devices: none -> 65.6 us  [gather_by_hops(): lax.ppermute(moving, mesh_axis, [(i, (i + 1) % size) for i in range(size)])]
    all_gather x1, waiting for transfers between devices: 58.4 us -> 0.01 us  [per_device(): lax.all_gather(full_rows, 'vocab', axis=0, tiled=True)]
    ppermute x0 -> x7, starting transfers between devices: none -> 19.5 us  [gather_by_hops(): lax.ppermute(moving, mesh_axis, [(i, (i + 1) % size) for i in range(size)])]
    unnamed x17 -> x42, local copies, waits for them, and re-layouts: 2.41 us -> 14 us
    unnamed x1, blocking collectives: 22.5 us -> 30 us
    all_to_all x1, blocking collectives: 9.6 us -> 14.7 us  [per_device(): lax.all_to_all(normed, 'width', split_axis=0, concat_axis=1, tiled=True)]
  transfers between devices with their start and end apart: 2 -> 8, of which waited for: 2 -> 4; matrix products, arithmetic and copies ran while one was open for 1% -> 4% of each run, Pallas kernels for 0% -> 0%
where the time goes in v1:
time: 465 us; the launch traced here: 464 us
  blocking collectives  317 us (68%)
  waiting for transfers between devices  65.6 us (14%)
  local copies, waits for them, and re-layouts  21.4 us (5%)
  starting transfers between devices  19.6 us (4%)
  between operations  15.1 us (3%)
  matrix products  12.9 us (3%)
  other arithmetic  9.19 us (2%)
    all_gather x4, blocking collectives, merged_2(): pieces = jax.tree.map(lambda part: lax.all_gather(part, axis), value)  152 us
    psum x1, blocking collectives, per_device(): lax.psum(partial_value, ('vocab', 'width')) / lengths.astype(jnp.float32)  96.1 us
    ppermute x7, waiting for transfers between devices, gather_by_hops(): lax.ppermute(moving, mesh_axis, [(i, (i + 1) % size) for i in range(size)])  65.6 us
    unnamed x1, blocking collectives  30 us
    psum x1, blocking collectives, per_device(): energy = lax.psum(jnp.sum(values * values, axis=1), 'width')  23.9 us
    ppermute x7, starting transfers between devices, gather_by_hops(): lax.ppermute(moving, mesh_axis, [(i, (i + 1) % size) for i in range(size)])  19.5 us
    all_to_all x1, blocking collectives, per_device(): lax.all_to_all(normed, 'width', split_axis=0, concat_axis=1, tiled=True)  14.7 us
    unnamed x42, local copies, waits for them, and re-layouts  14 us
  transfers between devices with their start and end apart: 8, of which 4 were waited for; matrix products, arithmetic and copies ran while one was open for 4% of the time, Pallas kernels for 0%

profile of v1, /device:TPU:1, one launch (start us, length us, event | category | flops | bytes accessed | tf_op | source)
XLA Modules:
  0.0 464.4 jit_solution(8162286199095943899)
XLA Ops:
  7.2 5.0 %collective-permute-start = (bf16[1600,256]{1,0:T(8,128)(2,1)}, bf16[1600,256]{1,0:T(8,128)(2,1)S(1)}, u32[]{:S(2)}, u32[]{:S(2)}) collective-permute-start(bf16[1600,256]{1,0:T(8,128)(2,1)} %param.12), channel_id=1, source_target_pairs={{0,1},{1,2},{2,3},{3,4},{4,5},{5,6},{6,7},{7,0},{8,9},{9,10},{10,1... | collective-permute-start | bytes 2457608 | tf_op jit(solution)/shard_map/ppermute | solution.py:14
  12.2 24.8 %collective-permute-done = bf16[1600,256]{1,0:T(8,128)(2,1)S(1)} collective-permute-done((bf16[1600,256]{1,0:T(8,128)(2,1)}, bf16[1600,256]{1,0:T(8,128)(2,1)S(1)}, u32[]{:S(2)}, u32[]{:S(2)}) %collective-permute-start) | collective-permute-done | bytes 819232 | tf_op jit(solution)/shard_map/ppermute | solution.py:14
  37.0 1.9 collective-permute-start.1
  40.5 23.9 %psum.14 = f32[128]{0:T(128)S(1)} all-reduce(f32[128]{0:T(128)S(1)} %fusion.5), channel_id=1, replica_groups=mesh['vocab'=64,'width'=8] {'width'}, use_global_device_ids=true, to_apply=%region_1.0 | all-reduce | flops 128 | bytes 1024 | tf_op jit(solution)/shard_map/psum | solution.py:54
  64.4 3.4 collective-permute-start.2
  68.7 14.7 %all_to_all.19 = bf16[8,16,256]{2,1,0:T(8,128)(2,1)S(1)} all-to-all(bf16[8,16,256]{2,1,0:T(8,128)(2,1)S(1)} %bitcast.73), channel_id=1, replica_groups=mesh['vocab'=64,'width'=8] {'width'}, dimensions={0} | all-to-all | bytes 131072 | tf_op jit(solution)/shard_map/all_to_all | solution.py:59
  84.1 2.5 collective-permute-start.3
  86.6 13.6 %collective-permute-done.3 = bf16[1600,256]{1,0:T(8,128)(2,1)S(1)} collective-permute-done((bf16[1600,256]{1,0:T(8,128)(2,1)S(1)}, bf16[1600,256]{1,0:T(8,128)(2,1)S(1)}, u32[]{:S(2)}, u32[]{:S(2)}) %collective-permute-start.3) | collective-permute-done | bytes 819232 | tf_op jit(solution)/shard_map/ppermute | solution.py:14
  101.1 2.2 collective-permute-start.4
  103.3 13.6 %collective-permute-done.4 = bf16[1600,256]{1,0:T(8,128)(2,1)S(1)} collective-permute-done((bf16[1600,256]{1,0:T(8,128)(2,1)S(1)}, bf16[1600,256]{1,0:T(8,128)(2,1)S(1)}, u32[]{:S(2)}, u32[]{:S(2)}) %collective-permute-start.4) | collective-permute-done | bytes 819232 | tf_op jit(solution)/shard_map/ppermute | solution.py:14
  117.9 2.2 collective-permute-start.5
  120.1 13.5 %collective-permute-done.5 = bf16[1600,256]{1,0:T(8,128)(2,1)} collective-permute-done((bf16[1600,256]{1,0:T(8,128)(2,1)S(1)}, bf16[1600,256]{1,0:T(8,128)(2,1)}, u32[]{:S(2)}, u32[]{:S(2)}) %collective-permute-start.5) | collective-permute-done | bytes 819232 | tf_op jit(solution)/shard_map/ppermute | solution.py:14
  133.6 2.4 collective-permute-start.6
  136.0 1.3 dynamic-slice
  138.8 30.0 %all-reduce = s32[1024]{0:T(1024)S(1)} all-reduce(s32[1024]{0:T(1024)S(1)} %dynamic-update-slice), channel_id=1, replica_groups=mesh['vocab'=64,'width'=8] {'vocab'}, use_global_device_ids=true, to_apply=%add | all-reduce | flops 1024 | bytes 8192
  170.5 1.4 constant_dynamic-update-slice_fusion.15
  171.9 1.3 constant_dynamic-update-slice_fusion.14
  173.1 1.3 constant_dynamic-update-slice_fusion.13
  176.0 1.3 constant_dynamic-update-slice_fusion.8
  177.3 1.3 constant_dynamic-update-slice_fusion.7
  180.5 3.4 constant_dynamic-slice_fusion.5
  183.9 16.2 %while.32 = (s32[]{:T(128)}, f32[2,512]{1,0:T(2,128)S(1)}, f32[2,512]{1,0:T(2,128)S(1)}, f32[2,512]{1,0:T(2,128)S(1)}, f32[2,512]{1,0:T(2,128)S(1)}, /*index=5*/...) while((s32[]{:T(128)}, f32[2,512]{1,0:T(2,128)S(1)}, ...), condition=%wide.region_7.8_spmd, body=%wide.region_2.7_spmd.sunk | while | flops 3361996288 | bytes 15250565 | solution.py:75
  183.9 6.5 %fusion.14 = (f32[512]{0:T(512)S(1)}, f32[512,1600]{0,1:T(8,128)S(1)}) fusion(bf16[1600,2048]{1,0:T(8,128)(2,1)} %get-tuple-element.320, bf16[2,512,2048]{2,1,0:T(8,128)(2,1)} %get-tuple-element.319, s32[]{:T(128)} %get-tuple-element.303), kind=kOutput, calls=%fused_computation.48.clone.1 | convolution fusion | flops 3356261888 | bytes 11930112 | tf_op jit(solution)/shard_map/while/body/eval_jaxpr/dot_general | solution.py:72
  190.4 1.4 fusion.15
  192.0 6.4 %fusion.14 = (f32[512]{0:T(512)S(1)}, f32[512,1600]{0,1:T(8,128)S(1)}) fusion(bf16[1600,2048]{1,0:T(8,128)(2,1)} %get-tuple-element.320, bf16[2,512,2048]{2,1,0:T(8,128)(2,1)} %get-tuple-element.319, s32[]{:T(128)} %get-tuple-element.303), kind=kOutput, calls=%fused_computation.48.clone.1 | convolution fusion | flops 3356261888 | bytes 11930112 | tf_op jit(solution)/shard_map/while/body/eval_jaxpr/dot_general | solution.py:72
  198.4 1.4 fusion.15
  200.1 40.8 %all-gather = f32[64,1,1024]{2,1,0:T(1,128)S(1)} all-gather(f32[1,1,1024]{2,1,0:T(1,128)S(1)} %reshape.60), channel_id=1, replica_groups=mesh['vocab'=64,'width'=8] {'vocab'}, dimensions={0}, use_global_device_ids=true | all-gather | bytes 266240 | tf_op jit(solution)/shard_map/all_gather | solution.py:21
  240.9 37.1 %all-gather.1 = f32[64,1,1024]{2,1,0:T(1,128)S(1)} all-gather(f32[1,1,1024]{2,1,0:T(1,128)S(1)} %reshape.62), channel_id=1, replica_groups=mesh['vocab'=64,'width'=8] {'vocab'}, dimensions={0}, use_global_device_ids=true | all-gather | bytes 266240 | tf_op jit(solution)/shard_map/all_gather | solution.py:21
  278.1 36.9 %all-gather.2 = f32[64,1,1024]{2,1,0:T(1,128)S(1)} all-gather(f32[1,1,1024]{2,1,0:T(1,128)S(1)} %reshape.64), channel_id=1, replica_groups=mesh['vocab'=64,'width'=8] {'vocab'}, dimensions={0}, use_global_device_ids=true | all-gather | bytes 266240 | tf_op jit(solution)/shard_map/all_gather | solution.py:21
  315.1 37.3 %all-gather.3 = f32[64,1,1024]{2,1,0:T(1,128)S(1)} all-gather(f32[1,1,1024]{2,1,0:T(1,128)S(1)} %reshape.66), channel_id=1, replica_groups=mesh['vocab'=64,'width'=8] {'vocab'}, dimensions={0}, use_global_device_ids=true | all-gather | bytes 266240 | tf_op jit(solution)/shard_map/all_gather | solution.py:21
  352.7 7.6 %while.33 = (s32[]{:T(128)}, f32[1024]{0:T(1024)S(1)}, f32[1024]{0:T(1024)S(1)}, f32[1024]{0:T(1024)S(1)}, f32[1024]{0:T(1024)S(1)}, /*index=5*/f32[63,1024]{1,0...) while((s32[]{:T(128)}, f32[1024]{0:T(1024)S(1)}, ...), condition=%wide.region_9.10_spmd, body=%wide.region_8.9_spmd.sunk | while | flops 16386 | bytes 110701 | solution.py:24
  360.9 96.1 %psum.15 = f32[64]{0:T(128)S(1)} all-reduce(f32[64]{0:T(128)S(1)} %select_reduce_fusion.1), channel_id=1, replica_groups=mesh['vocab'=64,'width'=8] {'vocab','width'}, use_global_device_ids=true, to_apply=%region_12.13 | all-reduce | flops 64 | bytes 512 | tf_op jit(solution)/shard_map/psum | solution.py:103
  (459 shorter events, 16.8 us)
Async XLA Ops:
  7.2 173.2 %copy-start = (bf16[1600,256]{1,0:T(8,128)(2,1)S(1)}, bf16[1600,256]{1,0:T(8,128)(2,1)}, u32[]{:S(2)}) copy-start(bf16[1600,256]{1,0:T(8,128)(2,1)} %param.12) | copy-start | bytes 2457604
  7.2 176.7 %all-gather.6.cloned.1.call-start = ((), (), s32[]{:S(2)}) async-start(), calls=%async_computation.1 | async-start | bytes 4259840 | tf_op jit(solution)/shard_map/all_gather | solution.py:61
  7.2 29.8 %collective-permute-start = (bf16[1600,256]{1,0:T(8,128)(2,1)}, bf16[1600,256]{1,0:T(8,128)(2,1)S(1)}, u32[]{:S(2)}, u32[]{:S(2)}) collective-permute-start(bf16[1600,256]{1,0:T(8,128)(2,1)} %param.12), channel_id=1, source_target_pairs={{0,1},{1,2},{2,3},{3,4},{4,5},{5,6},{6,7},{7,0},{8,9},{9,10},{10,1... | collective-permute-start | bytes 2457608 | tf_op jit(solution)/shard_map/ppermute | solution.py:14
  37.0 27.4 %collective-permute-start.1 = (bf16[1600,256]{1,0:T(8,128)(2,1)S(1)}, bf16[1600,256]{1,0:T(8,128)(2,1)S(1)}, u32[]{:S(2)}, u32[]{:S(2)}) collective-permute-start(bf16[1600,256]{1,0:T(8,128)(2,1)S(1)} %collective-permute-done), channel_id=1, source_target_pairs={{0,1},{1,2},{2,3},{3,4},{4,5},{5,6},{6,7},{7,0},{8,9},{9,10},{10,1... | collective-permute-start | bytes 2457608 | tf_op jit(solution)/shard_map/ppermute | solution.py:14
  64.4 19.6 %collective-permute-start.2 = (bf16[1600,256]{1,0:T(8,128)(2,1)S(1)}, bf16[1600,256]{1,0:T(8,128)(2,1)S(1)}, u32[]{:S(2)}, u32[]{:S(2)}) collective-permute-start(bf16[1600,256]{1,0:T(8,128)(2,1)S(1)} %collective-permute-done.1), channel_id=1, source_target_pairs={{0,1},{1,2},{2,3},{3,4},{4,5},{5,6},{6,7},{7,0},{8,9},{9,10},{10,1... | collective-permute-start | bytes 2457608 | tf_op jit(solution)/shard_map/ppermute | solution.py:14
  84.1 16.2 %collective-permute-start.3 = (bf16[1600,256]{1,0:T(8,128)(2,1)S(1)}, bf16[1600,256]{1,0:T(8,128)(2,1)S(1)}, u32[]{:S(2)}, u32[]{:S(2)}) collective-permute-start(bf16[1600,256]{1,0:T(8,128)(2,1)S(1)} %collective-permute-done.2), channel_id=1, source_target_pairs={{0,1},{1,2},{2,3},{3,4},{4,5},{5,6},{6,7},{7,0},{8,9},{9,10},{10,1... | collective-permute-start | bytes 2457608 | tf_op jit(solution)/shard_map/ppermute | solution.py:14
  100.3 0.9 copy-start.1
  101.1 15.8 %collective-permute-start.4 = (bf16[1600,256]{1,0:T(8,128)(2,1)S(1)}, bf16[1600,256]{1,0:T(8,128)(2,1)S(1)}, u32[]{:S(2)}, u32[]{:S(2)}) collective-permute-start(bf16[1600,256]{1,0:T(8,128)(2,1)S(1)} %collective-permute-done.3), channel_id=1, source_target_pairs={{0,1},{1,2},{2,3},{3,4},{4,5},{5,6},{6,7},{7,0},{8,9},{9,10},{10,1... | collective-permute-start | bytes 2457608 | tf_op jit(solution)/shard_map/ppermute | solution.py:14
  117.0 0.9 copy-start.3
  117.9 15.7 %collective-permute-start.5 = (bf16[1600,256]{1,0:T(8,128)(2,1)S(1)}, bf16[1600,256]{1,0:T(8,128)(2,1)}, u32[]{:S(2)}, u32[]{:S(2)}) collective-permute-start(bf16[1600,256]{1,0:T(8,128)(2,1)S(1)} %collective-permute-done.4), channel_id=1, source_target_pairs={{0,1},{1,2},{2,3},{3,4},{4,5},{5,6},{6,7},{7,0},{8,9},{9,10},{10,1... | collective-permute-start | bytes 2457608 | tf_op jit(solution)/shard_map/ppermute | solution.py:14
  133.6 36.9 %collective-permute-start.6 = (bf16[1600,256]{1,0:T(8,128)(2,1)}, bf16[1600,256]{1,0:T(8,128)(2,1)}, u32[]{:S(2)}, u32[]{:S(2)}) collective-permute-start(bf16[1600,256]{1,0:T(8,128)(2,1)} %collective-permute-done.5), channel_id=1, source_target_pairs={{0,1},{1,2},{2,3},{3,4},{4,5},{5,6},{6,7},{7,0},{8,9},{9,10},{10,1... | collective-permute-start | bytes 2457608 | tf_op jit(solution)/shard_map/ppermute | solution.py:14
  170.5 9.3 %copy-start.4 = (bf16[1600,256]{1,0:T(8,128)(2,1)S(1)}, bf16[1600,256]{1,0:T(8,128)(2,1)}, u32[]{:S(2)}) copy-start(bf16[1600,256]{1,0:T(8,128)(2,1)} %copy-done.3) | copy-start | bytes 2457604
  170.5 9.4 %copy-start.2 = (bf16[1600,256]{1,0:T(8,128)(2,1)S(1)}, bf16[1600,256]{1,0:T(8,128)(2,1)}, u32[]{:S(2)}) copy-start(bf16[1600,256]{1,0:T(8,128)(2,1)} %copy-done.1) | copy-start | bytes 2457604
  183.9 176.4 %copy-start.7 = (s32[16]{0:T(128)S(1)}, s32[16]{0:T(128)}, u32[]{:S(2)}) copy-start(s32[16]{0:T(128)} %param.14) | copy-start | bytes 196
  183.9 273.2 %copy-start.6 = (s32[64]{0:T(128)S(1)}, s32[64]{0:T(128)}, u32[]{:S(2)}) copy-start(s32[64]{0:T(128)} %param.15) | copy-start | bytes 772
  360.9 96.7 %copy-start.5 = (f32[16]{0:T(128)}, f32[16]{0:T(128)S(1)}, u32[]{:S(2)}) copy-start(f32[16]{0:T(128)S(1)} %get-tuple-element.158) | copy-start | bytes 196
Sparse Core Ops, SparseCore 0:
  84.2 90.0 all-gather.5
